TPU v7x, 32 devices: a whole 2x2x4 slice. The times are simulated.
32 devices in a mesh: seq: 8 (over y, x, core), head: 4 (over z).
Axes of the slice: x: 2, y: 2, z: 4, core: 2. Of those that a mesh axis runs over, the one named last changes fastest.
Arguments:
- lengths: int32 [16], replicated, may hold values from 1 to 1024, 2048 in all
- query: bfloat16 [2048, 8192], P('seq', 'head'), may hold values from -4.5 to 4.5
- keys: bfloat16 [2048, 1024], P('seq', 'head'), may hold values from -4.5 to 4.5
- values: bfloat16 [2048, 1024], P('seq', 'head'), may hold values from -6 to 6
- attention_grad: bfloat16 [2048, 8192], P('seq', 'head'), may hold values from -6 to 6
Outputs:
- attention_out: bfloat16 [2048, 8192], P('seq', 'head')
- query_grad: bfloat16 [2048, 8192], P('seq', 'head')
- key_grad: bfloat16 [2048, 1024], P('seq', 'head')
- value_grad: bfloat16 [2048, 1024], P('seq', 'head')
Inputs may be any that keep to these rules, and one draw needn't show every extreme that they name: The lengths sum to 2048 and the longest is exactly 1024.
All inputs are finite; a program needn't handle non-finite values.
Results may differ from a plain program's by a relative error of at most 0.023.
Values may be sent and summed in bfloat16 or wider, within the bound.
A program may use at most 128 MiB of HBM per device.

v0:
```python
import jax
import jax.numpy as jnp
from jax import lax
from jax.sharding import PartitionSpec as P

ATT_DIM = 128


masked_score = -1e30


def passed_along(block, axis, distance):
    devices = range(lax.axis_size(axis))
    route = [(i - distance, i) for i in devices if i - distance in devices]
    return lax.ppermute(block, axis, route)


def segment_of(position, ends):
    return jnp.sum((ends[None, :] <= position[:, None]).astype(jnp.int32), axis=1)


def on_device(lengths, query, keys, values, attention_grad):
    tok_rows = query.shape[0]
    seq_count = lax.axis_size("seq")
    device = lax.axis_index("seq")
    first = device * tok_rows
    heads = query.shape[1] // ATT_DIM
    kv_count = keys.shape[1] // ATT_DIM
    share = heads // kv_count
    scale = ATT_DIM ** (-0.5)
    ends = jnp.cumsum(lengths)
    local_pos = first + jnp.arange(tok_rows, dtype=jnp.int32)
    local_seg = segment_of(local_pos, ends)
    query_heads = query.reshape(tok_rows, kv_count, share, ATT_DIM)
    key_heads = keys.reshape(tok_rows, kv_count, ATT_DIM)
    value_heads = values.reshape(tok_rows, kv_count, ATT_DIM)
    grad_heads = attention_grad.reshape(tok_rows, kv_count, share, ATT_DIM)

    def permit(row_pos, row_seg, col_pos):
        col_seg = segment_of(col_pos, ends)
        return (
            (row_seg[:, None] == col_seg[None, :])
            & (row_pos[:, None] >= col_pos[None, :])
            & (col_pos[None, :] >= 0)
        )

    kv_pair = jnp.stack([keys, values])
    stats_init = (
        jnp.full((kv_count, share, tok_rows), masked_score, jnp.float32),
        jnp.zeros((kv_count, share, tok_rows), jnp.float32),
        jnp.zeros((tok_rows, kv_count, share, ATT_DIM), jnp.float32),
    )

    def key_step(carry, piece, stat_piece, start):
        rows = piece.shape[1]
        query_pos = start + jnp.arange(rows, dtype=jnp.int32)
        query_seg = segment_of(query_pos, ends)
        piece_query = piece[0].reshape(rows, kv_count, share, ATT_DIM)
        piece_grad = piece[1].reshape(rows, kv_count, share, ATT_DIM)
        piece_total = stat_piece[0].T.reshape(kv_count, share, rows)
        piece_delta = stat_piece[1].T.reshape(kv_count, share, rows)

        def work(state):
            key_accum, value_accum = state
            allow = permit(query_pos, query_seg, local_pos)[None, None]
            score = (
                jnp.einsum(
                    "tgqd,sgd->gqts", piece_query, key_heads, preferred_element_type=jnp.float32
                )
                * scale
            )
            prob = jnp.where(allow, jnp.exp(score - piece_total[..., None]), 0.0)
            dprob = jnp.einsum(
                "tgqd,sgd->gqts", piece_grad, value_heads, preferred_element_type=jnp.float32
            )
            dscore = (prob * (dprob - piece_delta[..., None]) * scale).astype(jnp.bfloat16)
            value_accum = value_accum + jnp.einsum(
                "gqts,tgqd->sgd",
                prob.astype(jnp.bfloat16),
                piece_grad,
                preferred_element_type=jnp.float32,
            )
            key_accum = key_accum + jnp.einsum(
                "gqts,tgqd->sgd", dscore, piece_query, preferred_element_type=jnp.float32
            )
            return (key_accum, value_accum)

        return work(carry)

    query_zero = jnp.zeros((tok_rows, kv_count, share, ATT_DIM), jnp.float32)
    key_zero = jnp.zeros((tok_rows, kv_count, ATT_DIM), jnp.float32)
    row_pair = jnp.stack([query, attention_grad])
    piece = lax.all_gather(kv_pair, "seq", axis=1, tiled=True)
    rows = piece.shape[1]
    key_pos = jnp.arange(rows, dtype=jnp.int32)
    piece_keys = piece[0].reshape(rows, kv_count, ATT_DIM)
    piece_values = piece[1].reshape(rows, kv_count, ATT_DIM)

    def work(state):
        top, mass, accum = state
        allow = permit(local_pos, local_seg, key_pos)[None, None]
        score = (
            jnp.einsum(
                "tgqd,sgd->gqts", query_heads, piece_keys, preferred_element_type=jnp.float32
            )
            * scale
        )
        score = jnp.where(allow, score, masked_score)
        top_new = jnp.maximum(top, jnp.max(score, axis=3))
        weight = jnp.where(allow, jnp.exp(score - top_new[..., None]), 0.0)
        mass_new = jnp.sum(weight, axis=3)
        update = jnp.einsum(
            "gqts,sgd->tgqd",
            weight.astype(jnp.bfloat16),
            piece_values,
            preferred_element_type=jnp.float32,
        )
        return (top_new, mass_new, update)

    stats = work(stats_init)
    top, mass, accum = stats
    log_total = top + jnp.log(mass)
    attn_out = accum / mass.transpose(2, 0, 1)[..., None]
    delta = jnp.sum(grad_heads.astype(jnp.float32) * attn_out, axis=3).transpose(1, 2, 0)
    log_total, delta, attn_out = (log_total, delta, attn_out)
    local_stats = jnp.stack(
        [log_total.reshape(heads, tok_rows).T, delta.reshape(heads, tok_rows).T]
    )
    piece = lax.all_gather(kv_pair, "seq", axis=1, tiled=True)
    rows = piece.shape[1]
    query_key_pos = jnp.arange(rows, dtype=jnp.int32)
    query_piece_keys = piece[0].reshape(rows, kv_count, ATT_DIM)
    query_piece_values = piece[1].reshape(rows, kv_count, ATT_DIM)

    def work(accum):
        allow = permit(local_pos, local_seg, query_key_pos)[None, None]
        score = (
            jnp.einsum(
                "tgqd,sgd->gqts", query_heads, query_piece_keys, preferred_element_type=jnp.float32
            )
            * scale
        )
        prob = jnp.where(allow, jnp.exp(score - log_total[..., None]), 0.0)
        dprob = jnp.einsum(
            "tgqd,sgd->gqts", grad_heads, query_piece_values, preferred_element_type=jnp.float32
        )
        dscore = (prob * (dprob - delta[..., None]) * scale).astype(jnp.bfloat16)
        return jnp.einsum(
            "gqts,sgd->tgqd", dscore, query_piece_keys, preferred_element_type=jnp.float32
        )

    query_accum = work(query_zero)
    key_start = key_step((key_zero, key_zero), row_pair, local_stats, first)

    def pass_along(turn, carry):
        moving, moving_stats, state = carry
        moving = passed_along(moving, "seq", -1)
        moving_stats = passed_along(moving_stats, "seq", -1)
        return (
            moving,
            moving_stats,
            key_step(state, moving, moving_stats, first + turn * tok_rows),
        )

    final_carry = lax.fori_loop(1, seq_count, pass_along, (row_pair, local_stats, key_start))
    key_state = final_carry[2]
    attention_out = attn_out.reshape(tok_rows, heads * ATT_DIM).astype(jnp.bfloat16)
    query_grad = query_accum.reshape(tok_rows, heads * ATT_DIM).astype(jnp.bfloat16)
    key_grad = key_state[0].reshape(tok_rows, kv_count * ATT_DIM).astype(jnp.bfloat16)
    value_grad = key_state[1].reshape(tok_rows, kv_count * ATT_DIM).astype(jnp.bfloat16)
    return (attention_out, query_grad, key_grad, value_grad)


def solution(mesh):
    in_specs = (P(), P("seq", "head"), P("seq", "head"), P("seq", "head"), P("seq", "head"))
    out_specs = (P("seq", "head"), P("seq", "head"), P("seq", "head"), P("seq", "head"))
    return jax.shard_map(
        on_device, mesh=mesh, in_specs=in_specs, out_specs=out_specs, check_vma=False
    )
```

profile of v0, /device:TPU:1, one launch (start us, length us, event | category | flops | bytes accessed | tf_op | source)
XLA Modules:
  0.0 399.5 jit_solution(10998054684208391461)
XLA Ops:
  12.5 2.3 copy.87
  16.2 2.7 pad_maximum_fusion
  18.9 2.8 fusion.73
  22.3 18.9 %all-gather.2.cloned.1.call-done = bf16[2,2048,256]{1,2,0:T(8,128)(2,1)} async-done(((bf16[2,256,256]{1,2,0:T(8,128)(2,1)}), bf16[2,2048,256]{1,2,0:T(8,128)(2,1)}) %all-gather.2.cloned.1.call-update) | async-done | bytes 2097168 | tf_op jit(solution)/shard_map/all_gather | solution.py:93
  42.9 13.7 %fusion.41 = (f32[2,8,256]{2,1,0:T(8,128)S(1)}, f32[2,2048,256,8]{2,1,3,0:T(8,128)}) fusion(pred[256,2048]{0,1:T(8,128)(4,1)S(1)} %fusion.60, bf16[2048,2,128,1]{0,2,3,1:T(8,128)(2,1)S(1)} %bitcast.266, bf16[256,2,8,128]{3,2,1,0:T(8,128)(2,1)S(1)} %bitcast.258), kind=kOutput, calls=%fused_computation.42 | convolution fusion | flops 2172645376 | bytes 36192256 | tf_op jit(solution)/shard_map/tgqd,sgd->gqts/dot_general | solution.py:103
  56.7 14.9 %fusion.42 = f32[2,8,256]{2,1,0:T(8,128)S(1)} fusion(f32[2,2048,256,8]{2,1,3,0:T(8,128)} %get-tuple-element.295, f32[2,8,256]{2,1,0:T(8,128)S(1)} %broadcast_maximum_fusion, pred[256,2048]{0,1:T(8,128)(4,1)S(1)} %fusion.60), kind=kLoop, calls=%fused_computation.43 | loop fusion | flops 41938944 | bytes 34111488 | tf_op jit(solution)/shard_map/reduce_sum | solution.py:111
  71.6 15.6 %multiply_reduce_fusion = (f32[256,2,8]{0,2,1:T(8,128)S(1)}, bf16[256,2,8,128]{0,3,2,1:T(8,128)(2,1)}) fusion(bf16[256,2048]{0,1:T(8,128)(2,1)S(1)} %copy.83, f32[256,2,8]{0,2,1:T(8,128)S(1)} %bitcast.280, bf16[2048,2,128,1]{0,2,3,1:T(8,128)(2,1)S(1)} %bitcast.276, f32[2,2048,256,8]{2,1,3,0:T(8,128)} %get-tuple-element.295, ...), kind=kOutput, calls=%fused_computation.60 | convolution fusion | flops 2192044032 | bytes 37273600 | tf_op jit(solution)/shard_map/gqts,sgd->tgqd/dot_general | solution.py:112
  87.2 2.3 copy.101
  89.4 18.6 %fusion.64 = bf16[2,128,8,256]{3,1,2,0:T(8,128)(2,1)} fusion(bf16[2048,2,128,1]{0,2,3,1:T(8,128)(2,1)} %bitcast.267, f32[2,2048,256,8]{2,1,3,0:T(8,128)} %get-tuple-element.295, f32[2,8,256]{2,1,0:T(8,128)S(1)} %bitcast.282, f32[2,8,256]{2,1,0:T(8,128)S(1)} %log_add_fusion, pred[256,2048]{0,1:T(8,128)(4,1)S(1)} %fusion.60, ...), kind=kOutput, calls=%fused_computation.65 | convolution fusion | flops 4354211840 | bytes 38305792 | tf_op jit(solution)/shard_map/gqts,sgd->tgqd/dot_general | solution.py:148
  108.0 2.3 copy.102
  110.3 3.7 fusion.68
  114.0 5.0 %fusion.71 = f32[256,2,128]{2,0,1:T(8,128)} fusion(f32[2,256,256,8]{2,1,3,0:T(8,128)} %fusion.73, bf16[256,2,128,1]{0,2,3,1:T(8,128)(2,1)S(1)} %bitcast.273, bf16[256,2,8,128]{0,3,2,1:T(8,128)(2,1)S(1)} %bitcast.264, f32[2,8,256]{2,1,0:T(8,128)S(1)} %bitcast.283, f32[2,8,256]{2,1,0:T(8,128)S(1)} %log_add_fusion, pred[256,256]{0,1:T(8,128)(4,1)S(1)} %and_and_fusion.1, ...), kind=kOutput, calls=%fused_computation.68 | convolution fusion | flops 544210944 | bytes 6782976 | tf_op jit(solution)/shard_map/gqts,tgqd->sgd/dot_general | solution.py:83
  119.0 271.2 %while.21 = (s32[]{:T(128)}, bf16[2,256,2048]{1,2,0:T(8,128)(2,1)}, f32[2,256,16]{1,2,0:T(8,128)S(1)}, f32[256,2,128]{2,0,1:T(8,128)}, f32[256,2,128]{2,0,1:T(8,...) while((s32[]{:T(128)}, bf16[2,256,2048]{1,2,0:T(8,128)(2,1)}, ...), condition=%wide.region_9.10_spmd.clone.clone, body=%wide.region_6.9_spmd.clone.clone.sunk | while | flops 1085694464 | bytes 58977196 | solution.py:165
  119.0 2.1 collective-permute-start
  121.2 1.9 collective-permute-start.1
  123.4 23.5 %collective-permute-done.1 = f32[2,256,16]{1,2,0:T(8,128)S(1)} collective-permute-done((f32[2,256,16]{1,2,0:T(8,128)S(1)}, f32[2,256,16]{1,2,0:T(8,128)S(1)}, u32[]{:S(2)}, u32[]{:S(2)}) %collective-permute-start.1) | collective-permute-done | bytes 32800 | tf_op jit(solution)/shard_map/while/body/eval_jaxpr/ppermute | solution.py:15
  147.8 1.9 copy-done
  151.4 5.1 %fusion.123 = f32[256,2,128]{2,0,1:T(8,128)} fusion(f32[256,2,128]{2,0,1:T(8,128)} %get-tuple-element.384, bf16[256,2,8,128]{0,3,2,1:T(8,128)(2,1)S(1)} %bitcast.254, f32[2,256,256,8]{2,1,3,0:T(8,128)} %copy-done, f32[2,8,256]{2,1,0:T(8,128)S(1)} %get-tuple-element.363, f32[2,8,256]{2,1,0:T(8,128)S(1)} %get-tuple-element.364, ...), kind=kOutput, calls=%fused_computation.16.clone.1 | convolution fusion | flops 544276480 | bytes 7045120 | tf_op jit(solution)/shard_map/while/body/eval_jaxpr/gqts,tgqd->sgd/dot_general | solution.py:83
  157.8 1.9 collective-permute-start
  159.7 1.9 collective-permute-start.1
  161.9 23.8 %collective-permute-done.1 = f32[2,256,16]{1,2,0:T(8,128)S(1)} collective-permute-done((f32[2,256,16]{1,2,0:T(8,128)S(1)}, f32[2,256,16]{1,2,0:T(8,128)S(1)}, u32[]{:S(2)}, u32[]{:S(2)}) %collective-permute-start.1) | collective-permute-done | bytes 32800 | tf_op jit(solution)/shard_map/while/body/eval_jaxpr/ppermute | solution.py:15
  186.6 1.9 copy-done
  190.1 5.1 %fusion.123 = f32[256,2,128]{2,0,1:T(8,128)} fusion(f32[256,2,128]{2,0,1:T(8,128)} %get-tuple-element.384, bf16[256,2,8,128]{0,3,2,1:T(8,128)(2,1)S(1)} %bitcast.254, f32[2,256,256,8]{2,1,3,0:T(8,128)} %copy-done, f32[2,8,256]{2,1,0:T(8,128)S(1)} %get-tuple-element.363, f32[2,8,256]{2,1,0:T(8,128)S(1)} %get-tuple-element.364, ...), kind=kOutput, calls=%fused_computation.16.clone.1 | convolution fusion | flops 544276480 | bytes 7045120 | tf_op jit(solution)/shard_map/while/body/eval_jaxpr/gqts,tgqd->sgd/dot_general | solution.py:83
  196.5 1.9 collective-permute-start
  198.4 1.9 collective-permute-start.1
  200.7 23.8 %collective-permute-done.1 = f32[2,256,16]{1,2,0:T(8,128)S(1)} collective-permute-done((f32[2,256,16]{1,2,0:T(8,128)S(1)}, f32[2,256,16]{1,2,0:T(8,128)S(1)}, u32[]{:S(2)}, u32[]{:S(2)}) %collective-permute-start.1) | collective-permute-done | bytes 32800 | tf_op jit(solution)/shard_map/while/body/eval_jaxpr/ppermute | solution.py:15
  225.3 1.9 copy-done
  228.8 5.1 %fusion.123 = f32[256,2,128]{2,0,1:T(8,128)} fusion(f32[256,2,128]{2,0,1:T(8,128)} %get-tuple-element.384, bf16[256,2,8,128]{0,3,2,1:T(8,128)(2,1)S(1)} %bitcast.254, f32[2,256,256,8]{2,1,3,0:T(8,128)} %copy-done, f32[2,8,256]{2,1,0:T(8,128)S(1)} %get-tuple-element.363, f32[2,8,256]{2,1,0:T(8,128)S(1)} %get-tuple-element.364, ...), kind=kOutput, calls=%fused_computation.16.clone.1 | convolution fusion | flops 544276480 | bytes 7045120 | tf_op jit(solution)/shard_map/while/body/eval_jaxpr/gqts,tgqd->sgd/dot_general | solution.py:83
  235.2 1.9 collective-permute-start
  237.2 1.9 collective-permute-start.1
  239.4 23.8 %collective-permute-done.1 = f32[2,256,16]{1,2,0:T(8,128)S(1)} collective-permute-done((f32[2,256,16]{1,2,0:T(8,128)S(1)}, f32[2,256,16]{1,2,0:T(8,128)S(1)}, u32[]{:S(2)}, u32[]{:S(2)}) %collective-permute-start.1) | collective-permute-done | bytes 32800 | tf_op jit(solution)/shard_map/while/body/eval_jaxpr/ppermute | solution.py:15
  264.0 1.9 copy-done
  267.6 5.1 %fusion.123 = f32[256,2,128]{2,0,1:T(8,128)} fusion(f32[256,2,128]{2,0,1:T(8,128)} %get-tuple-element.384, bf16[256,2,8,128]{0,3,2,1:T(8,128)(2,1)S(1)} %bitcast.254, f32[2,256,256,8]{2,1,3,0:T(8,128)} %copy-done, f32[2,8,256]{2,1,0:T(8,128)S(1)} %get-tuple-element.363, f32[2,8,256]{2,1,0:T(8,128)S(1)} %get-tuple-element.364, ...), kind=kOutput, calls=%fused_computation.16.clone.1 | convolution fusion | flops 544276480 | bytes 7045120 | tf_op jit(solution)/shard_map/while/body/eval_jaxpr/gqts,tgqd->sgd/dot_general | solution.py:83
  274.0 1.9 collective-permute-start
  275.9 1.9 collective-permute-start.1
  278.1 23.8 %collective-permute-done.1 = f32[2,256,16]{1,2,0:T(8,128)S(1)} collective-permute-done((f32[2,256,16]{1,2,0:T(8,128)S(1)}, f32[2,256,16]{1,2,0:T(8,128)S(1)}, u32[]{:S(2)}, u32[]{:S(2)}) %collective-permute-start.1) | collective-permute-done | bytes 32800 | tf_op jit(solution)/shard_map/while/body/eval_jaxpr/ppermute | solution.py:15
  302.8 1.9 copy-done
  306.3 5.1 %fusion.123 = f32[256,2,128]{2,0,1:T(8,128)} fusion(f32[256,2,128]{2,0,1:T(8,128)} %get-tuple-element.384, bf16[256,2,8,128]{0,3,2,1:T(8,128)(2,1)S(1)} %bitcast.254, f32[2,256,256,8]{2,1,3,0:T(8,128)} %copy-done, f32[2,8,256]{2,1,0:T(8,128)S(1)} %get-tuple-element.363, f32[2,8,256]{2,1,0:T(8,128)S(1)} %get-tuple-element.364, ...), kind=kOutput, calls=%fused_computation.16.clone.1 | convolution fusion | flops 544276480 | bytes 7045120 | tf_op jit(solution)/shard_map/while/body/eval_jaxpr/gqts,tgqd->sgd/dot_general | solution.py:83
  312.7 1.9 collective-permute-start
  314.7 1.9 collective-permute-start.1
  316.9 23.8 %collective-permute-done.1 = f32[2,256,16]{1,2,0:T(8,128)S(1)} collective-permute-done((f32[2,256,16]{1,2,0:T(8,128)S(1)}, f32[2,256,16]{1,2,0:T(8,128)S(1)}, u32[]{:S(2)}, u32[]{:S(2)}) %collective-permute-start.1) | collective-permute-done | bytes 32800 | tf_op jit(solution)/shard_map/while/body/eval_jaxpr/ppermute | solution.py:15
  341.5 1.9 copy-done
  345.1 5.1 %fusion.123 = f32[256,2,128]{2,0,1:T(8,128)} fusion(f32[256,2,128]{2,0,1:T(8,128)} %get-tuple-element.384, bf16[256,2,8,128]{0,3,2,1:T(8,128)(2,1)S(1)} %bitcast.254, f32[2,256,256,8]{2,1,3,0:T(8,128)} %copy-done, f32[2,8,256]{2,1,0:T(8,128)S(1)} %get-tuple-element.363, f32[2,8,256]{2,1,0:T(8,128)S(1)} %get-tuple-element.364, ...), kind=kOutput, calls=%fused_computation.16.clone.1 | convolution fusion | flops 544276480 | bytes 7045120 | tf_op jit(solution)/shard_map/while/body/eval_jaxpr/gqts,tgqd->sgd/dot_general | solution.py:83
  351.5 1.9 collective-permute-start
  353.4 1.9 collective-permute-start.1
  355.6 23.8 %collective-permute-done.1 = f32[2,256,16]{1,2,0:T(8,128)S(1)} collective-permute-done((f32[2,256,16]{1,2,0:T(8,128)S(1)}, f32[2,256,16]{1,2,0:T(8,128)S(1)}, u32[]{:S(2)}, u32[]{:S(2)}) %collective-permute-start.1) | collective-permute-done | bytes 32800 | tf_op jit(solution)/shard_map/while/body/eval_jaxpr/ppermute | solution.py:15
  380.3 1.9 copy-done
  383.8 5.1 %fusion.123 = f32[256,2,128]{2,0,1:T(8,128)} fusion(f32[256,2,128]{2,0,1:T(8,128)} %get-tuple-element.384, bf16[256,2,8,128]{0,3,2,1:T(8,128)(2,1)S(1)} %bitcast.254, f32[2,256,256,8]{2,1,3,0:T(8,128)} %copy-done, f32[2,8,256]{2,1,0:T(8,128)S(1)} %get-tuple-element.363, f32[2,8,256]{2,1,0:T(8,128)S(1)} %get-tuple-element.364, ...), kind=kOutput, calls=%fused_computation.16.clone.1 | convolution fusion | flops 544276480 | bytes 7045120 | tf_op jit(solution)/shard_map/while/body/eval_jaxpr/gqts,tgqd->sgd/dot_general | solution.py:83
  (171 shorter events, 39.7 us)
Async XLA Ops:
  7.2 7.6 %copy-start.2 = (bf16[256,2048]{1,0:T(8,128)(2,1)S(1)}, bf16[256,2048]{1,0:T(8,128)(2,1)}, u32[]{:S(2)}) copy-start(bf16[256,2048]{1,0:T(8,128)(2,1)} %param.8) | copy-start | bytes 3145732
  7.2 34.0 %all-gather.2.cloned.1.call-start = ((), (), s32[]{:S(2)}) async-start(), calls=%async_computation | async-start | bytes 2359296 | tf_op jit(solution)/shard_map/all_gather | solution.py:93
  42.9 13.8 %copy-start.3 = (bf16[1,2048,256]{1,2,0:T(8,128)(2,1)}, bf16[1,2048,256]{1,2,0:T(8,128)(2,1)S(1)}, u32[]{:S(2)}) copy-start(bf16[1,2048,256]{1,2,0:T(8,128)(2,1)S(1)} %get-tuple-element.292) | copy-start | bytes 3145732
  42.9 28.6 %copy-start.4 = (bf16[1,2048,256]{1,2,0:T(8,128)(2,1)}, bf16[1,2048,256]{1,2,0:T(8,128)(2,1)S(1)}, u32[]{:S(2)}) copy-start(bf16[1,2048,256]{1,2,0:T(8,128)(2,1)S(1)} %get-tuple-element.293) | copy-start | bytes 3145732
  119.0 27.9 %collective-permute-start = (bf16[2,256,2048]{1,2,0:T(8,128)(2,1)}, bf16[2,256,2048]{1,2,0:T(8,128)(2,1)S(1)}, u32[]{:S(2)}, u32[]{:S(2)}) collective-permute-start(bf16[2,256,2048]{1,2,0:T(8,128)(2,1)} %get-tuple-element.382), channel_id=1, source_target_pairs={{4,0},{8,4},{12,8},{16,12},{20,16},{24,20},{28,24},{5,1},{9,5},{13... | collective-permute-start | bytes 6291464 | tf_op jit(solution)/shard_map/while/body/eval_jaxpr/ppermute | solution.py:15
  121.2 25.7 %collective-permute-start.1 = (f32[2,256,16]{1,2,0:T(8,128)S(1)}, f32[2,256,16]{1,2,0:T(8,128)S(1)}, u32[]{:S(2)}, u32[]{:S(2)}) collective-permute-start(f32[2,256,16]{1,2,0:T(8,128)S(1)} %get-tuple-element.383), channel_id=1, source_target_pairs={{4,0},{8,4},{12,8},{16,12},{20,16},{24,20},{28,24},{5,1},{9,5},{13... | collective-permute-start | bytes 98312 | tf_op jit(solution)/shard_map/while/body/eval_jaxpr/ppermute | solution.py:15
  146.9 2.8 copy-start.5
  147.1 3.5 copy-start.1
  147.8 1.9 copy-start
  147.8 3.6 copy-start.7
  157.8 27.9 %collective-permute-start = (bf16[2,256,2048]{1,2,0:T(8,128)(2,1)}, bf16[2,256,2048]{1,2,0:T(8,128)(2,1)S(1)}, u32[]{:S(2)}, u32[]{:S(2)}) collective-permute-start(bf16[2,256,2048]{1,2,0:T(8,128)(2,1)} %get-tuple-element.382), channel_id=1, source_target_pairs={{4,0},{8,4},{12,8},{16,12},{20,16},{24,20},{28,24},{5,1},{9,5},{13... | collective-permute-start | bytes 6291464 | tf_op jit(solution)/shard_map/while/body/eval_jaxpr/ppermute | solution.py:15
  159.7 26.0 %collective-permute-start.1 = (f32[2,256,16]{1,2,0:T(8,128)S(1)}, f32[2,256,16]{1,2,0:T(8,128)S(1)}, u32[]{:S(2)}, u32[]{:S(2)}) collective-permute-start(f32[2,256,16]{1,2,0:T(8,128)S(1)} %get-tuple-element.383), channel_id=1, source_target_pairs={{4,0},{8,4},{12,8},{16,12},{20,16},{24,20},{28,24},{5,1},{9,5},{13... | collective-permute-start | bytes 98312 | tf_op jit(solution)/shard_map/while/body/eval_jaxpr/ppermute | solution.py:15
  185.7 2.8 copy-start.5
  185.8 3.5 copy-start.1
  186.5 1.9 copy-start
  186.5 3.6 copy-start.7
  189.4 0.7 copy-start.6
  196.5 27.9 %collective-permute-start = (bf16[2,256,2048]{1,2,0:T(8,128)(2,1)}, bf16[2,256,2048]{1,2,0:T(8,128)(2,1)S(1)}, u32[]{:S(2)}, u32[]{:S(2)}) collective-permute-start(bf16[2,256,2048]{1,2,0:T(8,128)(2,1)} %get-tuple-element.382), channel_id=1, source_target_pairs={{4,0},{8,4},{12,8},{16,12},{20,16},{24,20},{28,24},{5,1},{9,5},{13... | collective-permute-start | bytes 6291464 | tf_op jit(solution)/shard_map/while/body/eval_jaxpr/ppermute | solution.py:15
  198.4 26.0 %collective-permute-start.1 = (f32[2,256,16]{1,2,0:T(8,128)S(1)}, f32[2,256,16]{1,2,0:T(8,128)S(1)}, u32[]{:S(2)}, u32[]{:S(2)}) collective-permute-start(f32[2,256,16]{1,2,0:T(8,128)S(1)} %get-tuple-element.383), channel_id=1, source_target_pairs={{4,0},{8,4},{12,8},{16,12},{20,16},{24,20},{28,24},{5,1},{9,5},{13... | collective-permute-start | bytes 98312 | tf_op jit(solution)/shard_map/while/body/eval_jaxpr/ppermute | solution.py:15
  224.4 2.8 copy-start.5
  224.6 3.5 copy-start.1
  225.3 1.9 copy-start
  225.3 3.6 copy-start.7
  235.2 27.9 %collective-permute-start = (bf16[2,256,2048]{1,2,0:T(8,128)(2,1)}, bf16[2,256,2048]{1,2,0:T(8,128)(2,1)S(1)}, u32[]{:S(2)}, u32[]{:S(2)}) collective-permute-start(bf16[2,256,2048]{1,2,0:T(8,128)(2,1)} %get-tuple-element.382), channel_id=1, source_target_pairs={{4,0},{8,4},{12,8},{16,12},{20,16},{24,20},{28,24},{5,1},{9,5},{13... | collective-permute-start | bytes 6291464 | tf_op jit(solution)/shard_map/while/body/eval_jaxpr/ppermute | solution.py:15
  237.2 26.0 %collective-permute-start.1 = (f32[2,256,16]{1,2,0:T(8,128)S(1)}, f32[2,256,16]{1,2,0:T(8,128)S(1)}, u32[]{:S(2)}, u32[]{:S(2)}) collective-permute-start(f32[2,256,16]{1,2,0:T(8,128)S(1)} %get-tuple-element.383), channel_id=1, source_target_pairs={{4,0},{8,4},{12,8},{16,12},{20,16},{24,20},{28,24},{5,1},{9,5},{13... | collective-permute-start | bytes 98312 | tf_op jit(solution)/shard_map/while/body/eval_jaxpr/ppermute | solution.py:15
  263.2 2.8 copy-start.5
  263.3 3.5 copy-start.1
  264.0 1.9 copy-start
  264.0 3.6 copy-start.7
  274.0 27.9 %collective-permute-start = (bf16[2,256,2048]{1,2,0:T(8,128)(2,1)}, bf16[2,256,2048]{1,2,0:T(8,128)(2,1)S(1)}, u32[]{:S(2)}, u32[]{:S(2)}) collective-permute-start(bf16[2,256,2048]{1,2,0:T(8,128)(2,1)} %get-tuple-element.382), channel_id=1, source_target_pairs={{4,0},{8,4},{12,8},{16,12},{20,16},{24,20},{28,24},{5,1},{9,5},{13... | collective-permute-start | bytes 6291464 | tf_op jit(solution)/shard_map/while/body/eval_jaxpr/ppermute | solution.py:15
  275.9 26.0 %collective-permute-start.1 = (f32[2,256,16]{1,2,0:T(8,128)S(1)}, f32[2,256,16]{1,2,0:T(8,128)S(1)}, u32[]{:S(2)}, u32[]{:S(2)}) collective-permute-start(f32[2,256,16]{1,2,0:T(8,128)S(1)} %get-tuple-element.383), channel_id=1, source_target_pairs={{4,0},{8,4},{12,8},{16,12},{20,16},{24,20},{28,24},{5,1},{9,5},{13... | collective-permute-start | bytes 98312 | tf_op jit(solution)/shard_map/while/body/eval_jaxpr/ppermute | solution.py:15
  301.9 2.8 copy-start.5
  302.1 3.5 copy-start.1
  302.8 1.9 copy-start
  302.8 3.6 copy-start.7
  312.7 27.9 %collective-permute-start = (bf16[2,256,2048]{1,2,0:T(8,128)(2,1)}, bf16[2,256,2048]{1,2,0:T(8,128)(2,1)S(1)}, u32[]{:S(2)}, u32[]{:S(2)}) collective-permute-start(bf16[2,256,2048]{1,2,0:T(8,128)(2,1)} %get-tuple-element.382), channel_id=1, source_target_pairs={{4,0},{8,4},{12,8},{16,12},{20,16},{24,20},{28,24},{5,1},{9,5},{13... | collective-permute-start | bytes 6291464 | tf_op jit(solution)/shard_map/while/body/eval_jaxpr/ppermute | solution.py:15
  314.7 26.0 %collective-permute-start.1 = (f32[2,256,16]{1,2,0:T(8,128)S(1)}, f32[2,256,16]{1,2,0:T(8,128)S(1)}, u32[]{:S(2)}, u32[]{:S(2)}) collective-permute-start(f32[2,256,16]{1,2,0:T(8,128)S(1)} %get-tuple-element.383), channel_id=1, source_target_pairs={{4,0},{8,4},{12,8},{16,12},{20,16},{24,20},{28,24},{5,1},{9,5},{13... | collective-permute-start | bytes 98312 | tf_op jit(solution)/shard_map/while/body/eval_jaxpr/ppermute | solution.py:15
  340.7 2.8 copy-start.5
  340.8 3.5 copy-start.1
  341.5 1.9 copy-start
  341.5 3.6 copy-start.7
  351.5 27.9 %collective-permute-start = (bf16[2,256,2048]{1,2,0:T(8,128)(2,1)}, bf16[2,256,2048]{1,2,0:T(8,128)(2,1)S(1)}, u32[]{:S(2)}, u32[]{:S(2)}) collective-permute-start(bf16[2,256,2048]{1,2,0:T(8,128)(2,1)} %get-tuple-element.382), channel_id=1, source_target_pairs={{4,0},{8,4},{12,8},{16,12},{20,16},{24,20},{28,24},{5,1},{9,5},{13... | collective-permute-start | bytes 6291464 | tf_op jit(solution)/shard_map/while/body/eval_jaxpr/ppermute | solution.py:15
  353.4 26.0 %collective-permute-start.1 = (f32[2,256,16]{1,2,0:T(8,128)S(1)}, f32[2,256,16]{1,2,0:T(8,128)S(1)}, u32[]{:S(2)}, u32[]{:S(2)}) collective-permute-start(f32[2,256,16]{1,2,0:T(8,128)S(1)} %get-tuple-element.383), channel_id=1, source_target_pairs={{4,0},{8,4},{12,8},{16,12},{20,16},{24,20},{28,24},{5,1},{9,5},{13... | collective-permute-start | bytes 98312 | tf_op jit(solution)/shard_map/while/body/eval_jaxpr/ppermute | solution.py:15
  379.4 2.8 copy-start.5
  379.6 3.5 copy-start.1
  380.3 1.9 copy-start
  380.3 3.6 copy-start.7
  383.1 0.7 copy-start.6
  (5 other events, 3.6 us)
Sparse Core Ops, SparseCore 0:
  10.5 30.6 all-gather.1
where the time goes:
time: 406 us; the launch traced here: 400 us
  waiting for transfers between devices  185 us (46%)
  matrix products  106 us (26%)
  local copies, waits for them, and re-layouts  43.8 us (11%)
  starting transfers between devices  27.1 us (7%)
  other arithmetic  22.3 us (5%)
  between operations  14.2 us (3%)
    ppermute x14, waiting for transfers between devices, passed_along(): return lax.ppermute(block, axis, route)  166 us
    dot_general x8, matrix products, work(): jnp.einsum('gqts,tgqd->sgd', dscore, piece_query, preferred_element_type=...  40.7 us
    while x84, local copies, waits for them, and re-layouts  27.5 us
    ppermute x14, starting transfers between devices, passed_along(): return lax.ppermute(block, axis, route)  27 us
    all_gather x1, waiting for transfers between devices, on_device(): piece = lax.all_gather(kv_pair, 'seq', axis=1, tiled=True)  18.9 us
    dot_general x1, matrix products, work(): jnp.einsum('gqts,sgd->tgqd', dscore, query_piece_keys, preferred_element_...  18.6 us
    dot_general x1, matrix products, work(): jnp.einsum('gqts,sgd->tgqd', weight.astype(jnp.bfloat16), piece_values, p...  15.6 us
    reduce_sum x1, other arithmetic, work(): mass_new = jnp.sum(weight, axis=3)  14.9 us
  transfers between devices with their start and end apart: 15, of which 8 were waited for; matrix products, arithmetic and copies ran while one was open for 4% of the time, Pallas kernels for 0%

commit v1 on v0

v1 whole, which is shorter than its diff:
```python
import functools

import jax
import jax.numpy as jnp
from jax import lax
from jax.experimental import pallas as pl
from jax.experimental.pallas import tpu as pltpu
from jax.sharding import PartitionSpec as P

ATT_DIM = 128
LOG2E = 1.4426950408889634
MASKED = -1.0e30
MESH = pl.DeviceIdType.MESH

F32 = jnp.float32
BF16 = jnp.bfloat16
NT = (((1,), (1,)), ((), ()))
NN = (((1,), (0,)), ((), ()))


def kernel(
    n, span, kv_count, share,
    lengths, query, keys, values, grad,
    out, query_grad, key_grad, value_grad,
    kv, key_t, value_t, score, prob, dscore, acc, own, sent, got,
    gather_send, gather_recv, back_send, back_recv,
):
    rows = query.shape[0]
    scale = ATT_DIM ** -0.5
    me = lax.axis_index("seq")

    barrier = pltpu.get_barrier_semaphore()
    for k in range(1, span):
        @pl.when(me + k < n)
        def _():
            pl.semaphore_signal(barrier, inc=1, device_id={"seq": me + k}, device_id_type=MESH)

        @pl.when(me - k >= 0)
        def _():
            pl.semaphore_signal(barrier, inc=1, device_id={"seq": me - k}, device_id_type=MESH)

    def stage(g, _):
        columns = pl.ds(pl.multiple_of(g * ATT_DIM, ATT_DIM), ATT_DIM)
        kv[g, 0, 0] = keys[:, columns]
        kv[g, 0, 1] = values[:, columns]
        for k in range(1, span):
            @pl.when(me - k < 0)
            def _():
                kv[g, k] = jnp.zeros((2, rows, ATT_DIM), BF16)
        return 0

    lax.fori_loop(0, kv_count, stage, 0)
    pl.semaphore_wait(
        barrier, jnp.minimum(me, span - 1) + jnp.minimum(n - 1 - me, span - 1)
    )

    def gather(g, k):
        return pltpu.make_async_remote_copy(
            src_ref=kv.at[g, 0],
            dst_ref=kv.at[g, k],
            send_sem=gather_send.at[g, k],
            recv_sem=gather_recv.at[g, k],
            device_id={"seq": me + k},
            device_id_type=MESH,
        )

    def back(g, k):
        return pltpu.make_async_remote_copy(
            src_ref=sent.at[g, k],
            dst_ref=got.at[g, k],
            send_sem=back_send.at[g, k],
            recv_sem=back_recv.at[g, k],
            device_id={"seq": me - k},
            device_id_type=MESH,
        )

    def send_all(g, _):
        for k in range(1, span):
            @pl.when(me + k < n)
            def _():
                gather(g, k).start()
        return 0

    lax.fori_loop(0, kv_count, send_all, 0)

    q_lane = lax.broadcasted_iota(jnp.int32, (1, rows), 1)
    position = q_lane + me * rows
    start = jnp.zeros((1, rows), jnp.int32)
    end = 0
    for i in range(lengths.shape[0]):
        end = end + lengths[i]
        start = jnp.where(position >= end, end, start)

    def group(g, _):
        for k in range(1, span):
            @pl.when(me - k >= 0)
            def _():
                gather(g, k).wait_recv()
        for k in range(span):
            key_t[:, k * rows:(k + 1) * rows] = kv[g, k, 0].T
            value_t[:, k * rows:(k + 1) * rows] = kv[g, k, 1].T
        acc[...] = jnp.zeros_like(acc)

        def head(i, _):
            columns = pl.ds(pl.multiple_of((g * share + i) * ATT_DIM, ATT_DIM), ATT_DIM)
            q = query[:, columns]
            top = jnp.full((1, rows), MASKED, F32)
            k_row = lax.broadcasted_iota(jnp.int32, (rows, rows), 0)
            for k in range(span):
                s = lax.dot_general(kv[g, k, 0], q, NT, preferred_element_type=F32)
                allow = k_row >= start - (me - k) * rows
                if k == 0:
                    allow = allow & (k_row <= q_lane)
                s = jnp.where(allow, s, MASKED)
                score[k * rows:(k + 1) * rows, :] = s
                top = jnp.maximum(top, jnp.max(s, axis=0, keepdims=True))
            mass = jnp.zeros((1, rows), F32)
            for k in range(span):
                at = slice(k * rows, (k + 1) * rows)
                p = jnp.exp2((score[at, :] - top) * (scale * LOG2E))
                mass = mass + jnp.sum(p, axis=0, keepdims=True)
                score[at, :] = p
                prob[at, :] = p.astype(BF16)
            inverse = 1.0 / mass
            out_t = lax.dot_general(value_t[...], prob[...], NN, preferred_element_type=F32)
            out_t = out_t * inverse
            out[:, columns] = out_t.T.astype(BF16)
            grad_t = grad[:, columns].astype(F32).T
            factor = inverse * scale
            delta = jnp.sum(grad_t * out_t, axis=0, keepdims=True) * factor
            grad_t = grad_t * factor
            grad_s = grad_t.T.astype(BF16)
            grad_t = grad_t.astype(BF16)
            for k in range(span):
                at = slice(k * rows, (k + 1) * rows)
                dp = lax.dot_general(kv[g, k, 1], grad_t, NN, preferred_element_type=F32)
                dscore[at, :] = (score[at, :] * (dp - delta)).astype(BF16)
            acc[1] += lax.dot_general(prob[...], grad_s, NN, preferred_element_type=F32)
            acc[0] += lax.dot_general(dscore[...], q, NN, preferred_element_type=F32)
            dq = lax.dot_general(key_t[...], dscore[...], NN, preferred_element_type=F32)
            query_grad[:, columns] = dq.T.astype(BF16)
            return 0

        lax.fori_loop(0, share, head, 0)
        for k in range(1, span):
            @pl.when(me - k >= 0)
            def _():
                sent[g, k, 0] = acc[0, k * rows:(k + 1) * rows, :].astype(BF16)
                sent[g, k, 1] = (acc[1, k * rows:(k + 1) * rows, :] * (1.0 / scale)).astype(BF16)
                back(g, k).start()
        own[g, 0] = acc[0, 0:rows, :]
        own[g, 1] = acc[1, 0:rows, :] * (1.0 / scale)
        return 0

    lax.fori_loop(0, kv_count, group, 0)

    def finish(g, _):
        columns = pl.ds(pl.multiple_of(g * ATT_DIM, ATT_DIM), ATT_DIM)
        for k in range(1, span):
            @pl.when(me + k < n)
            def _():
                back(g, k).wait_recv()
                own[g] = own[g] + got[g, k].astype(F32)
        key_grad[:, columns] = own[g, 0].astype(BF16)
        value_grad[:, columns] = own[g, 1].astype(BF16)
        for k in range(1, span):
            @pl.when(me + k < n)
            def _():
                gather(g, k).wait_send()

            @pl.when(me - k >= 0)
            def _():
                back(g, k).wait_send()
        return 0

    lax.fori_loop(0, kv_count, finish, 0)


def on_device(lengths, query, keys, values, attention_grad):
    n = lax.axis_size("seq")
    rows = query.shape[0]
    kv_count = keys.shape[1] // ATT_DIM
    share = query.shape[1] // keys.shape[1]
    span = n // 2 + 1
    whole = pl.BlockSpec(memory_space=pltpu.VMEM)
    return pl.pallas_call(
        functools.partial(kernel, n, span, kv_count, share),
        out_shape=[
            jax.ShapeDtypeStruct(a.shape, BF16) for a in (query, query, keys, values)
        ],
        in_specs=[pl.BlockSpec(memory_space=pltpu.SMEM)] + [whole] * 4,
        out_specs=[whole] * 4,
        scratch_shapes=[
            pltpu.VMEM((kv_count, span, 2, rows, ATT_DIM), BF16),
            pltpu.VMEM((ATT_DIM, span * rows), BF16),
            pltpu.VMEM((ATT_DIM, span * rows), BF16),
            pltpu.VMEM((span * rows, rows), F32),
            pltpu.VMEM((span * rows, rows), BF16),
            pltpu.VMEM((span * rows, rows), BF16),
            pltpu.VMEM((2, span * rows, ATT_DIM), F32),
            pltpu.VMEM((kv_count, 2, rows, ATT_DIM), F32),
            pltpu.VMEM((kv_count, span, 2, rows, ATT_DIM), BF16),
            pltpu.VMEM((kv_count, span, 2, rows, ATT_DIM), BF16),
            pltpu.SemaphoreType.DMA((kv_count, span)),
            pltpu.SemaphoreType.DMA((kv_count, span)),
            pltpu.SemaphoreType.DMA((kv_count, span)),
            pltpu.SemaphoreType.DMA((kv_count, span)),
        ],
        compiler_params=pltpu.CompilerParams(
            collective_id=0, has_side_effects=True, vmem_limit_bytes=48 << 20
        ),
    )(lengths, query, keys, values, attention_grad)


def solution(mesh):
    in_specs = (P(), P("seq", "head"), P("seq", "head"), P("seq", "head"), P("seq", "head"))
    out_specs = (P("seq", "head"), P("seq", "head"), P("seq", "head"), P("seq", "head"))
    return jax.shard_map(
        on_device, mesh=mesh, in_specs=in_specs, out_specs=out_specs, check_vma=False
    )
```

time: 406 us -> 62.4 us (0.15); the launches traced: 400 us -> 61.6 us
  waiting for transfers between devices: 185 us -> 0 us
  matrix products: 106 us -> 0 us
  Pallas kernels: 0 us -> 52.8 us
  local copies, waits for them, and re-layouts: 43.8 us -> 8.16 us
  starting transfers between devices: 27.1 us -> 0 us
  other arithmetic: 22.3 us -> 0 us
  between operations: 14.2 us -> 0.65 us
    ppermute x14 -> x0, waiting for transfers between devices: 166 us -> none  [passed_along(): return lax.ppermute(block, axis, route)]
    dot_general x27 -> x0, matrix products: 106 us -> none  [the longest x8 40.7 us: work(): jnp.einsum('gqts,tgqd->sgd', dscore, piece_query, preferred_element_type=...]
    pallas_call x0 -> x1, Pallas kernels: none -> 52.8 us  [on_device(): pl.pallas_call(functools.partial(kernel, n, span, kv_count, share), out_s...]
    while x84 -> x0, local copies, waits for them, and re-layouts: 27.5 us -> none
    ppermute x14 -> x0, starting transfers between devices: 27 us -> none  [passed_along(): return lax.ppermute(block, axis, route)]
    all_gather x1 -> x0, waiting for transfers between devices: 18.9 us -> none  [on_device(): piece = lax.all_gather(kv_pair, 'seq', axis=1, tiled=True)]
    reduce_sum x10 -> x0, other arithmetic: 15.7 us -> none  [the longest x1 14.9 us: work(): mass_new = jnp.sum(weight, axis=3)]
    unnamed x15 -> x14, local copies, waits for them, and re-layouts: 11.5 us -> 8.16 us
  transfers between devices with their start and end apart: 15 -> 0, of which waited for: 8 -> 0; matrix products, arithmetic and copies ran while one was open for 4% -> 0% of each run, Pallas kernels for 0% -> 0%
where the time goes in v1:
time: 62.4 us; the launch traced here: 61.6 us
  Pallas kernels  52.8 us (85%)
  local copies, waits for them, and re-layouts  8.16 us (13%)
  between operations  0.65 us (1%)
    pallas_call x1, Pallas kernels, on_device(): pl.pallas_call(functools.partial(kernel, n, span, kv_count, share), out_s...  52.8 us
    unnamed x14, local copies, waits for them, and re-layouts  8.16 us

profile of v1, /device:TPU:1, one launch (start us, length us, event | category | flops | bytes accessed | tf_op | source)
XLA Modules:
  0.0 61.6 jit_solution(10650392001823145289)
XLA Ops:
  0.6 0.0 copy-start
  0.6 1.2 %copy-done = bf16[256,2048]{1,0:T(8,128)(2,1)S(1)} copy-done((bf16[256,2048]{1,0:T(8,128)(2,1)S(1)}, bf16[256,2048]{1,0:T(8,128)(2,1)}, u32[]{:S(2)}) %copy-start) | copy-done | bytes 1048600
  1.9 0.0 copy-start.1
  1.9 1.2 %copy-done.1 = bf16[256,2048]{1,0:T(8,128)(2,1)S(1)} copy-done((bf16[256,2048]{1,0:T(8,128)(2,1)S(1)}, bf16[256,2048]{1,0:T(8,128)(2,1)}, u32[]{:S(2)}) %copy-start.1) | copy-done | bytes 1048600
  3.1 0.0 copy-start.2
  3.1 0.9 %copy-done.2 = bf16[256,256]{1,0:T(8,128)(2,1)S(1)} copy-done((bf16[256,256]{1,0:T(8,128)(2,1)S(1)}, bf16[256,256]{1,0:T(8,128)(2,1)}, u32[]{:S(2)}) %copy-start.2) | copy-done | bytes 131096
  4.0 0.0 copy-start.3
  4.0 0.9 %copy-done.3 = bf16[256,256]{1,0:T(8,128)(2,1)S(1)} copy-done((bf16[256,256]{1,0:T(8,128)(2,1)S(1)}, bf16[256,256]{1,0:T(8,128)(2,1)}, u32[]{:S(2)}) %copy-start.3) | copy-done | bytes 131096
  4.9 0.0 copy-start.4
  4.9 0.7 %copy-done.4 = s32[16]{0:T(128)S(1)} copy-done((s32[16]{0:T(128)S(1)}, s32[16]{0:T(128)}, u32[]{:S(2)}) %copy-start.4) | copy-done | bytes 88
  5.5 52.8 %shard_map.84 = (bf16[256,2048]{1,0:T(8,128)(2,1)S(1)}, bf16[256,2048]{1,0:T(8,128)(2,1)S(1)}, bf16[256,256]{1,0:T(8,128)(2,1)S(1)}, bf16[256,256]{1,0:T(8,128)(2,1)S(1)}) custom-call(s32[16]{0:T(128)S(1)} %copy-done.4, bf16[256,2048]{1,0:T(8,128)(2,1)S(1)} %copy-done, bf16[256,256]{1,0:T(8,128)(2,1)S(1)} %copy-done.2, bf16[256,256]{1,0:T(8,128)(2,1)S(1)} %copy-done.3, ...), custom_call_target="tpu_custom_call" | custom-call | tf_op jit(solution)/shard_map/pallas_call | solution.py:186
  58.4 1.0 %copy.13 = bf16[256,2048]{1,0:T(8,128)(2,1)} copy(bf16[256,2048]{1,0:T(8,128)(2,1)S(1)} %get-tuple-element.8) | data formatting | bytes 2097152
  59.3 1.0 %copy.14 = bf16[256,2048]{1,0:T(8,128)(2,1)} copy(bf16[256,2048]{1,0:T(8,128)(2,1)S(1)} %get-tuple-element.9) | data formatting | bytes 2097152
  60.3 0.7 %copy.15 = bf16[256,256]{1,0:T(8,128)(2,1)} copy(bf16[256,256]{1,0:T(8,128)(2,1)S(1)} %get-tuple-element.10) | data formatting | bytes 262144
  61.0 0.7 %copy.16 = bf16[256,256]{1,0:T(8,128)(2,1)} copy(bf16[256,256]{1,0:T(8,128)(2,1)S(1)} %get-tuple-element.11) | data formatting | bytes 262144
Async XLA Ops:
  0.6 1.2 %copy-start = (bf16[256,2048]{1,0:T(8,128)(2,1)S(1)}, bf16[256,2048]{1,0:T(8,128)(2,1)}, u32[]{:S(2)}) copy-start(bf16[256,2048]{1,0:T(8,128)(2,1)} %query.1) | copy-start | bytes 3145732
  1.9 1.2 %copy-start.1 = (bf16[256,2048]{1,0:T(8,128)(2,1)S(1)}, bf16[256,2048]{1,0:T(8,128)(2,1)}, u32[]{:S(2)}) copy-start(bf16[256,2048]{1,0:T(8,128)(2,1)} %grad.1) | copy-start | bytes 3145732
  3.1 0.9 %copy-start.2 = (bf16[256,256]{1,0:T(8,128)(2,1)S(1)}, bf16[256,256]{1,0:T(8,128)(2,1)}, u32[]{:S(2)}) copy-start(bf16[256,256]{1,0:T(8,128)(2,1)} %keys.1) | copy-start | bytes 393220
  4.0 0.9 %copy-start.3 = (bf16[256,256]{1,0:T(8,128)(2,1)S(1)}, bf16[256,256]{1,0:T(8,128)(2,1)}, u32[]{:S(2)}) copy-start(bf16[256,256]{1,0:T(8,128)(2,1)} %values.1) | copy-start | bytes 393220
  4.9 0.7 %copy-start.4 = (s32[16]{0:T(128)S(1)}, s32[16]{0:T(128)}, u32[]{:S(2)}) copy-start(s32[16]{0:T(128)} %lengths.1) | copy-start | bytes 196

commit v2 on v1

v2 whole, which is shorter than its diff:
```python
import functools

import jax
import jax.numpy as jnp
from jax import lax
from jax.experimental import pallas as pl
from jax.experimental.pallas import tpu as pltpu
from jax.sharding import PartitionSpec as P

ATT_DIM = 128
LOG2E = 1.4426950408889634
MASKED = -1.0e30
MESH = pl.DeviceIdType.MESH

F32 = jnp.float32
BF16 = jnp.bfloat16
NT = (((1,), (1,)), ((), ()))
NN = (((1,), (0,)), ((), ()))


def kernel(
    n, span, kv_count, share, lead,
    lengths, query_hbm, keys, values, grad_hbm,
    out, query_grad, key_grad, value_grad,
    query, grad, kv, key_t, value_t, score, prob, dscore, acc, sent, mix, got,
    load, gather_send, gather_recv, back_send, mix_recv, back_recv,
):
    rows = query.shape[0]
    scale = ATT_DIM ** -0.5
    me = lax.axis_index("seq")
    odd = lax.rem(me, 2)
    pair = me + 1 - 2 * odd
    far = span // 2

    def load_kv(g, which):
        columns = pl.ds(pl.multiple_of(g * ATT_DIM, ATT_DIM), ATT_DIM)
        source = (keys, values)[which]
        return pltpu.make_async_copy(
            source.at[:, columns], kv.at[g, 0, which], load.at[2 + 2 * g + which]
        )

    def start_load(g, _):
        load_kv(g, 0).start()
        load_kv(g, 1).start()
        return 0

    lax.fori_loop(0, kv_count, start_load, 0)
    load_query = pltpu.make_async_copy(query_hbm, query, load.at[0])
    load_grad = pltpu.make_async_copy(grad_hbm, grad, load.at[1])
    load_query.start()
    load_grad.start()

    def signal(barrier, target):
        pl.semaphore_signal(barrier, inc=1, device_id={"seq": target}, device_id_type=MESH)

    barrier = pltpu.get_barrier_semaphore()
    signal(barrier, pair)
    for j in range(1, far + 1):
        @pl.when(me + 2 * j < n)
        def _():
            signal(barrier, me + 2 * j)

        @pl.when(me - 2 * j >= 0)
        def _():
            signal(barrier, me - 2 * j)

    def clear(g, _):
        for k in range(1, span):
            @pl.when(me - k < 0)
            def _():
                kv[g, k] = jnp.zeros((2, rows, ATT_DIM), BF16)
        return 0

    lax.fori_loop(0, kv_count, clear, 0)
    pl.semaphore_wait(
        barrier, 1 + jnp.minimum(me // 2, far) + jnp.minimum((n - 1 - me) // 2, far)
    )

    def remote(source, target, send_sem, recv_sem, device):
        return pltpu.make_async_remote_copy(
            src_ref=source, dst_ref=target, send_sem=send_sem, recv_sem=recv_sem,
            device_id={"seq": device}, device_id_type=MESH,
        )

    def gather(g, j):
        return remote(
            kv.at[g, 0], kv.at[g, 2 * j], gather_send.at[g, 2 * j],
            gather_recv.at[g, 2 * j], me + 2 * j,
        )

    def hand_on(g, j, slot):
        return remote(
            kv.at[g, 2 * j], kv.at[g, slot], gather_send.at[g, slot],
            gather_recv.at[g, slot], pair,
        )

    def each_hand_on(first, last, act):
        for j in range(first, last + 1):
            if j >= 1:
                @pl.when((odd == 1) & (me - 2 * j >= 0))
                def _():
                    act(j, 2 * j - 1)
            if j < far:
                @pl.when((odd == 0) & (me - 2 * j >= 0))
                def _():
                    act(j, 2 * j + 1)

    def begin(g, _):
        load_kv(g, 0).wait()
        load_kv(g, 1).wait()
        for j in range(1, far + 1):
            @pl.when(me + 2 * j < n)
            def _():
                gather(g, j).start()
        each_hand_on(0, 0, lambda j, slot: hand_on(g, j, slot).start())
        return 0

    lax.fori_loop(0, kv_count, begin, 0)

    def pass_on(g):
        for j in range(1, far + 1):
            @pl.when(me - 2 * j >= 0)
            def _():
                gather(g, j).wait_recv()
            each_hand_on(j, j, lambda j, slot: hand_on(g, j, slot).start())

    def partial(g, k):
        at = slice(k * rows, (k + 1) * rows)
        return acc[g, 0, at, :], acc[g, 1, at, :] * (1.0 / scale)

    def to_pair(g, k, j):
        return remote(
            sent.at[g, k], mix.at[g, j], back_send.at[g, k], mix_recv.at[g, j], pair
        )

    def back(g, j):
        return remote(
            sent.at[g, 2 * j], got.at[g, j], back_send.at[g, 2 * j],
            back_recv.at[g, j], me - 2 * j,
        )

    def each_to_pair(act):
        for k in range(1, span, 2):
            @pl.when((odd == 1) & (me - k >= 0))
            def _():
                act(k, (k - 1) // 2)

            @pl.when((odd == 0) & (me - k >= 0))
            def _():
                act(k, (k + 1) // 2)

    def share_partial(g):
        def act(k, j):
            dk, dv = partial(g, k)
            sent[g, k, 0] = dk.astype(BF16)
            sent[g, k, 1] = dv.astype(BF16)
            to_pair(g, k, j).start()

        each_to_pair(act)

    def wait_mix(g, j):
        to_pair(g, 1, j).wait_recv()

    def combine(g):
        for j in range(far, 0, -1):
            def relay(mixed):
                dk, dv = partial(g, 2 * j)
                if mixed:
                    wait_mix(g, j)
                    dk = dk + mix[g, j, 0].astype(F32)
                    dv = dv + mix[g, j, 1].astype(F32)
                sent[g, 2 * j, 0] = dk.astype(BF16)
                sent[g, 2 * j, 1] = dv.astype(BF16)
                back(g, j).start()

            if j < far:
                @pl.when(me - 2 * j >= 0)
                def _():
                    relay(True)
            else:
                @pl.when((me - 2 * j >= 0) & (odd == 1))
                def _():
                    relay(True)

                @pl.when((me - 2 * j >= 0) & (odd == 0))
                def _():
                    relay(False)

    q_lane = lax.broadcasted_iota(jnp.int32, (1, rows), 1)
    position = q_lane + me * rows
    start = jnp.zeros((1, rows), jnp.int32)
    end = 0
    for i in range(lengths.shape[0]):
        end = end + lengths[i]
        start = jnp.where(position >= end, end, start)

    load_query.wait()
    load_grad.wait()
    pass_on(0)
    steps = share // lead

    def group(g, _):
        for k in range(1, span, 2):
            @pl.when(me - k >= 0)
            def _():
                hand_on(g, 0, k).wait_recv()
        for k in range(span):
            key_t[:, k * rows:(k + 1) * rows] = kv[g, k, 0].T
            value_t[:, k * rows:(k + 1) * rows] = kv[g, k, 1].T
        acc[g] = jnp.zeros(acc.shape[1:], F32)

        def one(i, slot):
            sc, pr, ds = score.at[slot], prob.at[slot], dscore.at[slot]
            columns = pl.ds(pl.multiple_of((g * share + i) * ATT_DIM, ATT_DIM), ATT_DIM)
            q = query[:, columns]
            top = jnp.full((1, rows), MASKED, F32)
            k_row = lax.broadcasted_iota(jnp.int32, (rows, rows), 0)
            for k in range(span):
                s = lax.dot_general(kv[g, k, 0], q, NT, preferred_element_type=F32)
                allow = k_row >= start - (me - k) * rows
                if k == 0:
                    allow = allow & (k_row <= q_lane)
                s = jnp.where(allow, s, MASKED)
                sc[k * rows:(k + 1) * rows, :] = s
                top = jnp.maximum(top, jnp.max(s, axis=0, keepdims=True))
            yield
            mass = jnp.zeros((1, rows), F32)
            for k in range(span):
                at = slice(k * rows, (k + 1) * rows)
                p = jnp.exp2((sc[at, :] - top) * (scale * LOG2E))
                mass = mass + jnp.sum(p, axis=0, keepdims=True)
                sc[at, :] = p
                pr[at, :] = p.astype(BF16)
            inverse = 1.0 / mass
            out_t = lax.dot_general(value_t[...], pr[...], NN, preferred_element_type=F32)
            out_t = out_t * inverse
            out[:, columns] = out_t.T.astype(BF16)
            grad_t = grad[:, columns].astype(F32).T
            factor = inverse * scale
            delta = jnp.sum(grad_t * out_t, axis=0, keepdims=True) * factor
            grad_t = grad_t * factor
            grad_s = grad_t.T.astype(BF16)
            grad_t = grad_t.astype(BF16)
            yield
            for k in range(span):
                at = slice(k * rows, (k + 1) * rows)
                dp = lax.dot_general(kv[g, k, 1], grad_t, NN, preferred_element_type=F32)
                ds[at, :] = (sc[at, :] * (dp - delta)).astype(BF16)
            acc[g, 1] += lax.dot_general(pr[...], grad_s, NN, preferred_element_type=F32)
            yield
            acc[g, 0] += lax.dot_general(ds[...], q, NN, preferred_element_type=F32)
            dq = lax.dot_general(key_t[...], ds[...], NN, preferred_element_type=F32)
            query_grad[:, columns] = dq.T.astype(BF16)
            yield

        def head(i, _):
            if kv_count > 1:
                @pl.when((i == min(1, steps - 1)) & (g >= 1))
                def _():
                    combine(g - 1)

                @pl.when((i == steps // 2) & (g + 1 < kv_count))
                def _():
                    pass_on(g + 1)
            runs = [one(lead * i + slot, slot) for slot in range(lead)]
            for _ in range(4):
                for run in runs:
                    next(run)
            return 0

        lax.fori_loop(0, steps, head, 0)
        share_partial(g)
        return 0

    lax.fori_loop(0, kv_count, group, 0)
    combine(kv_count - 1)

    def finish(g, _):
        columns = pl.ds(pl.multiple_of(g * ATT_DIM, ATT_DIM), ATT_DIM)

        @pl.when(odd == 0)
        def _():
            wait_mix(g, 0)
            acc[g, 0, 0:rows, :] += mix[g, 0, 0].astype(F32)
            acc[g, 1, 0:rows, :] += mix[g, 0, 1].astype(F32) * scale

        for j in range(1, far + 1):
            @pl.when(me + 2 * j < n)
            def _():
                back(g, j).wait_recv()
                acc[g, 0, 0:rows, :] += got[g, j, 0].astype(F32)
                acc[g, 1, 0:rows, :] += got[g, j, 1].astype(F32) * scale
        dk, dv = partial(g, 0)
        key_grad[:, columns] = dk.astype(BF16)
        value_grad[:, columns] = dv.astype(BF16)
        for j in range(1, far + 1):
            @pl.when(me + 2 * j < n)
            def _():
                gather(g, j).wait_send()

            @pl.when(me - 2 * j >= 0)
            def _():
                back(g, j).wait_send()
        each_hand_on(0, far, lambda j, slot: hand_on(g, j, slot).wait_send())
        each_to_pair(lambda k, j: to_pair(g, k, j).wait_send())
        return 0

    lax.fori_loop(0, kv_count, finish, 0)


def on_device(lengths, query, keys, values, attention_grad):
    n = lax.axis_size("seq")
    rows = query.shape[0]
    kv_count = keys.shape[1] // ATT_DIM
    share = query.shape[1] // keys.shape[1]
    span = n // 2 + 1
    lead = 2
    whole = pl.BlockSpec(memory_space=pltpu.VMEM)
    block = (2, rows, ATT_DIM)
    return pl.pallas_call(
        functools.partial(kernel, n, span, kv_count, share, lead),
        out_shape=[
            jax.ShapeDtypeStruct(a.shape, BF16) for a in (query, query, keys, values)
        ],
        in_specs=[pl.BlockSpec(memory_space=pltpu.SMEM)]
        + [pl.BlockSpec(memory_space=pl.ANY)] * 4,
        out_specs=[whole] * 4,
        scratch_shapes=[
            pltpu.VMEM(query.shape, BF16),
            pltpu.VMEM(query.shape, BF16),
            pltpu.VMEM((kv_count, span) + block, BF16),
            pltpu.VMEM((ATT_DIM, span * rows), BF16),
            pltpu.VMEM((ATT_DIM, span * rows), BF16),
            pltpu.VMEM((lead, span * rows, rows), F32),
            pltpu.VMEM((lead, span * rows, rows), BF16),
            pltpu.VMEM((lead, span * rows, rows), BF16),
            pltpu.VMEM((kv_count, 2, span * rows, ATT_DIM), F32),
            pltpu.VMEM((kv_count, span) + block, BF16),
            pltpu.VMEM((kv_count, span // 2 + 1) + block, BF16),
            pltpu.VMEM((kv_count, span // 2 + 1) + block, BF16),
            pltpu.SemaphoreType.DMA((2 + 2 * kv_count,)),
            pltpu.SemaphoreType.DMA((kv_count, span)),
            pltpu.SemaphoreType.DMA((kv_count, span)),
            pltpu.SemaphoreType.DMA((kv_count, span)),
            pltpu.SemaphoreType.DMA((kv_count, span // 2 + 1)),
            pltpu.SemaphoreType.DMA((kv_count, span // 2 + 1)),
        ],
        compiler_params=pltpu.CompilerParams(
            collective_id=0, has_side_effects=True, vmem_limit_bytes=60 << 20
        ),
    )(lengths, query, keys, values, attention_grad)


def solution(mesh):
    in_specs = (P(), P("seq", "head"), P("seq", "head"), P("seq", "head"), P("seq", "head"))
    out_specs = (P("seq", "head"), P("seq", "head"), P("seq", "head"), P("seq", "head"))
    return jax.shard_map(
        on_device, mesh=mesh, in_specs=in_specs, out_specs=out_specs, check_vma=False
    )
```

time: 62.4 us -> 49.3 us (0.79)
  Pallas kernels: 52.8 us -> 43.4 us
  local copies, waits for them, and re-layouts: 8.16 us -> 5.02 us
    pallas_call x1, Pallas kernels: 52.8 us -> 43.4 us  [on_device(): pl.pallas_call(functools.partial(kernel, n, span, kv_count, share, lead),...]
    unnamed x14 -> x10, local copies, waits for them, and re-layouts: 8.16 us -> 5.02 us
where the time goes in v2:
time: 49.3 us; the launch traced here: 49.1 us
  Pallas kernels  43.4 us (88%)
  local copies, waits for them, and re-layouts  5.02 us (10%)
  between operations  0.65 us (1%)
    pallas_call x1, Pallas kernels, on_device(): pl.pallas_call(functools.partial(kernel, n, span, kv_count, share, lead),...  43.4 us
    unnamed x10, local copies, waits for them, and re-layouts  5.02 us

profile of v2, /device:TPU:1, one launch (start us, length us, event | category | flops | bytes accessed | tf_op | source)
XLA Modules:
  0.0 49.1 jit_solution(2123289488080684198)
XLA Ops:
  0.6 43.4 %shard_map.84 = (bf16[256,2048]{1,0:T(8,128)(2,1)}, bf16[256,2048]{1,0:T(8,128)(2,1)}, bf16[256,256]{1,0:T(8,128)(2,1)}, bf16[256,256]{1,0:T(8,128)(2,1)}) custom-call(s32[16]{0:T(128)} %lengths.1, bf16[256,2048]{1,0:T(8,128)(2,1)} %query_hbm.1, bf16[256,256]{1,0:T(8,128)(2,1)} %keys.1, bf16[256,256]{1,0:T(8,128)(2,1)} %values.1, bf16[256,2048]{1,0:T(8,128)(2,1)} %grad_hbm.1), custom_call_target="tpu_custom_call" | custom-call | tf_op jit(solution)/shard_map/pallas_call | solution.py:320
  44.1 0.0 copy-start
  44.1 2.4 %copy.13 = bf16[256,2048]{1,0:T(8,128)(2,1)} copy(bf16[256,2048]{1,0:T(8,128)(2,1)} %get-tuple-element.8) | data formatting | bytes 2097152
  46.5 0.0 copy-done
  46.5 0.0 copy-start.2
  46.5 1.0 %copy.14 = bf16[256,2048]{1,0:T(8,128)(2,1)} copy(bf16[256,2048]{1,0:T(8,128)(2,1)S(1)} %copy-done) | data formatting | bytes 2097152
  47.4 0.1 copy-done.2
  47.5 0.0 copy-start.1
  47.5 0.7 %copy.15 = bf16[256,256]{1,0:T(8,128)(2,1)} copy(bf16[256,256]{1,0:T(8,128)(2,1)S(1)} %copy-done.2) | data formatting | bytes 262144
  48.2 0.3 copy-done.1
  48.4 0.7 %copy.16 = bf16[256,256]{1,0:T(8,128)(2,1)} copy(bf16[256,256]{1,0:T(8,128)(2,1)S(1)} %copy-done.1) | data formatting | bytes 262144
Async XLA Ops:
  44.1 2.4 %copy-start = (bf16[256,2048]{1,0:T(8,128)(2,1)S(1)}, bf16[256,2048]{1,0:T(8,128)(2,1)}, u32[]{:S(2)}) copy-start(bf16[256,2048]{1,0:T(8,128)(2,1)} %get-tuple-element.9) | copy-start | bytes 3145732
  46.5 1.0 %copy-start.2 = (bf16[256,256]{1,0:T(8,128)(2,1)S(1)}, bf16[256,256]{1,0:T(8,128)(2,1)}, u32[]{:S(2)}) copy-start(bf16[256,256]{1,0:T(8,128)(2,1)} %get-tuple-element.10) | copy-start | bytes 393220
  47.5 1.0 %copy-start.1 = (bf16[256,256]{1,0:T(8,128)(2,1)S(1)}, bf16[256,256]{1,0:T(8,128)(2,1)}, u32[]{:S(2)}) copy-start(bf16[256,256]{1,0:T(8,128)(2,1)} %get-tuple-element.11) | copy-start | bytes 393220

commit v3 on v2

--- a/solution.py
+++ b/solution.py
@@ -105,7 +105,7 @@
                 def _():
                     act(j, 2 * j + 1)
 
-    def begin(g, _):
+    def begin(g):
         load_kv(g, 0).wait()
         load_kv(g, 1).wait()
         for j in range(1, far + 1):
@@ -113,9 +113,8 @@
             def _():
                 gather(g, j).start()
         each_hand_on(0, 0, lambda j, slot: hand_on(g, j, slot).start())
-        return 0
-
-    lax.fori_loop(0, kv_count, begin, 0)
+
+    begin(0)
 
     def pass_on(g):
         for j in range(1, far + 1):
@@ -208,6 +207,10 @@
             key_t[:, k * rows:(k + 1) * rows] = kv[g, k, 0].T
             value_t[:, k * rows:(k + 1) * rows] = kv[g, k, 1].T
         acc[g] = jnp.zeros(acc.shape[1:], F32)
+        if kv_count > 1:
+            @pl.when(g + 1 < kv_count)
+            def _():
+                begin(g + 1)
 
         def one(i, slot):
             sc, pr, ds = score.at[slot], prob.at[slot], dscore.at[slot]
@@ -259,7 +262,7 @@
                 def _():
                     combine(g - 1)
 
-                @pl.when((i == steps // 2) & (g + 1 < kv_count))
+                @pl.when((i == steps - 1) & (g + 1 < kv_count))
                 def _():
                     pass_on(g + 1)
             runs = [one(lead * i + slot, slot) for slot in range(lead)]

time: 49.3 us -> 46.6 us (0.945)
  Pallas kernels: 43.4 us -> 40.7 us
    pallas_call x1, Pallas kernels: 43.4 us -> 40.7 us  [on_device(): pl.pallas_call(functools.partial(kernel, n, span, kv_count, share, lead),...]
where the time goes in v3:
time: 46.6 us; the launch traced here: 46.4 us
  Pallas kernels  40.7 us (87%)
  local copies, waits for them, and re-layouts  5.02 us (11%)
  between operations  0.65 us (1%)
    pallas_call x1, Pallas kernels, on_device(): pl.pallas_call(functools.partial(kernel, n, span, kv_count, share, lead),...  40.7 us
    unnamed x10, local copies, waits for them, and re-layouts  5.02 us

profile of v3, /device:TPU:1, one launch (start us, length us, event | category | flops | bytes accessed | tf_op | source)
XLA Modules:
  0.0 46.4 jit_solution(13188650900787134341)
XLA Ops:
  0.6 40.7 %shard_map.84 = (bf16[256,2048]{1,0:T(8,128)(2,1)}, bf16[256,2048]{1,0:T(8,128)(2,1)}, bf16[256,256]{1,0:T(8,128)(2,1)}, bf16[256,256]{1,0:T(8,128)(2,1)}) custom-call(s32[16]{0:T(128)} %lengths.1, bf16[256,2048]{1,0:T(8,128)(2,1)} %query_hbm.1, bf16[256,256]{1,0:T(8,128)(2,1)} %keys.1, bf16[256,256]{1,0:T(8,128)(2,1)} %values.1, bf16[256,2048]{1,0:T(8,128)(2,1)} %grad_hbm.1), custom_call_target="tpu_custom_call" | custom-call | tf_op jit(solution)/shard_map/pallas_call | solution.py:323
  41.3 0.0 copy-start
  41.3 2.4 %copy.13 = bf16[256,2048]{1,0:T(8,128)(2,1)} copy(bf16[256,2048]{1,0:T(8,128)(2,1)} %get-tuple-element.8) | data formatting | bytes 2097152
  43.7 0.0 copy-done
  43.7 0.0 copy-start.2
  43.7 1.0 %copy.14 = bf16[256,2048]{1,0:T(8,128)(2,1)} copy(bf16[256,2048]{1,0:T(8,128)(2,1)S(1)} %copy-done) | data formatting | bytes 2097152
  44.7 0.1 copy-done.2
  44.8 0.0 copy-start.1
  44.8 0.7 %copy.15 = bf16[256,256]{1,0:T(8,128)(2,1)} copy(bf16[256,256]{1,0:T(8,128)(2,1)S(1)} %copy-done.2) | data formatting | bytes 262144
  45.4 0.3 copy-done.1
  45.7 0.7 %copy.16 = bf16[256,256]{1,0:T(8,128)(2,1)} copy(bf16[256,256]{1,0:T(8,128)(2,1)S(1)} %copy-done.1) | data formatting | bytes 262144
Async XLA Ops:
  41.3 2.4 %copy-start = (bf16[256,2048]{1,0:T(8,128)(2,1)S(1)}, bf16[256,2048]{1,0:T(8,128)(2,1)}, u32[]{:S(2)}) copy-start(bf16[256,2048]{1,0:T(8,128)(2,1)} %get-tuple-element.9) | copy-start | bytes 3145732
  43.7 1.0 %copy-start.2 = (bf16[256,256]{1,0:T(8,128)(2,1)S(1)}, bf16[256,256]{1,0:T(8,128)(2,1)}, u32[]{:S(2)}) copy-start(bf16[256,256]{1,0:T(8,128)(2,1)} %get-tuple-element.10) | copy-start | bytes 393220
  44.8 1.0 %copy-start.1 = (bf16[256,256]{1,0:T(8,128)(2,1)S(1)}, bf16[256,256]{1,0:T(8,128)(2,1)}, u32[]{:S(2)}) copy-start(bf16[256,256]{1,0:T(8,128)(2,1)} %get-tuple-element.11) | copy-start | bytes 393220

commit v4 on v3

--- a/solution.py
+++ b/solution.py
@@ -317,7 +317,7 @@
     kv_count = keys.shape[1] // ATT_DIM
     share = query.shape[1] // keys.shape[1]
     span = n // 2 + 1
-    lead = 2
+    lead = 4
     whole = pl.BlockSpec(memory_space=pltpu.VMEM)
     block = (2, rows, ATT_DIM)
     return pl.pallas_call(

time: 46.6 us -> 45 us (0.966); the launches traced: 46.4 us -> 44.2 us
  Pallas kernels: 40.7 us -> 38.6 us
    pallas_call x1, Pallas kernels: 40.7 us -> 38.6 us  [on_device(): pl.pallas_call(functools.partial(kernel, n, span, kv_count, share, lead),...]
where the time goes in v4:
time: 45 us; the launch traced here: 44.2 us
  Pallas kernels  38.6 us (86%)
  local copies, waits for them, and re-layouts  5.02 us (11%)
  between operations  0.65 us (1%)
    pallas_call x1, Pallas kernels, on_device(): pl.pallas_call(functools.partial(kernel, n, span, kv_count, share, lead),...  38.6 us
    unnamed x10, local copies, waits for them, and re-layouts  5.02 us

profile of v4, /device:TPU:1, one launch (start us, length us, event | category | flops | bytes accessed | tf_op | source)
XLA Modules:
  0.0 44.2 jit_solution(14872759054305276877)
XLA Ops:
  0.6 38.6 %shard_map.84 = (bf16[256,2048]{1,0:T(8,128)(2,1)}, bf16[256,2048]{1,0:T(8,128)(2,1)}, bf16[256,256]{1,0:T(8,128)(2,1)}, bf16[256,256]{1,0:T(8,128)(2,1)}) custom-call(s32[16]{0:T(128)} %lengths.1, bf16[256,2048]{1,0:T(8,128)(2,1)} %query_hbm.1, bf16[256,256]{1,0:T(8,128)(2,1)} %keys.1, bf16[256,256]{1,0:T(8,128)(2,1)} %values.1, bf16[256,2048]{1,0:T(8,128)(2,1)} %grad_hbm.1), custom_call_target="tpu_custom_call" | custom-call | tf_op jit(solution)/shard_map/pallas_call | solution.py:323
  39.2 0.0 copy-start
  39.2 2.4 %copy.13 = bf16[256,2048]{1,0:T(8,128)(2,1)} copy(bf16[256,2048]{1,0:T(8,128)(2,1)} %get-tuple-element.8) | data formatting | bytes 2097152
  41.6 0.0 copy-done
  41.6 0.0 copy-start.2
  41.6 1.0 %copy.14 = bf16[256,2048]{1,0:T(8,128)(2,1)} copy(bf16[256,2048]{1,0:T(8,128)(2,1)S(1)} %copy-done) | data formatting | bytes 2097152
  42.6 0.1 copy-done.2
  42.6 0.0 copy-start.1
  42.6 0.7 %copy.15 = bf16[256,256]{1,0:T(8,128)(2,1)} copy(bf16[256,256]{1,0:T(8,128)(2,1)S(1)} %copy-done.2) | data formatting | bytes 262144
  43.3 0.3 copy-done.1
  43.6 0.7 %copy.16 = bf16[256,256]{1,0:T(8,128)(2,1)} copy(bf16[256,256]{1,0:T(8,128)(2,1)S(1)} %copy-done.1) | data formatting | bytes 262144
Async XLA Ops:
  39.2 2.4 %copy-start = (bf16[256,2048]{1,0:T(8,128)(2,1)S(1)}, bf16[256,2048]{1,0:T(8,128)(2,1)}, u32[]{:S(2)}) copy-start(bf16[256,2048]{1,0:T(8,128)(2,1)} %get-tuple-element.9) | copy-start | bytes 3145732
  41.6 1.0 %copy-start.2 = (bf16[256,256]{1,0:T(8,128)(2,1)S(1)}, bf16[256,256]{1,0:T(8,128)(2,1)}, u32[]{:S(2)}) copy-start(bf16[256,256]{1,0:T(8,128)(2,1)} %get-tuple-element.10) | copy-start | bytes 393220
  42.6 1.0 %copy-start.1 = (bf16[256,256]{1,0:T(8,128)(2,1)S(1)}, bf16[256,256]{1,0:T(8,128)(2,1)}, u32[]{:S(2)}) copy-start(bf16[256,256]{1,0:T(8,128)(2,1)} %get-tuple-element.11) | copy-start | bytes 393220

commit v5 on v4

--- a/solution.py
+++ b/solution.py
@@ -139,7 +139,7 @@
         )
 
     def each_to_pair(act):
-        for k in range(1, span, 2):
+        for k in range(span - 2, 0, -2):
             @pl.when((odd == 1) & (me - k >= 0))
             def _():
                 act(k, (k - 1) // 2)

time: 45 us -> 45 us (level)
  no operation moved by 1% of the time
where the time goes in v5:
time: 45 us; the launch traced here: 44.2 us
  Pallas kernels  38.6 us (86%)
  local copies, waits for them, and re-layouts  5.02 us (11%)
  between operations  0.65 us (1%)
    pallas_call x1, Pallas kernels, on_device(): pl.pallas_call(functools.partial(kernel, n, span, kv_count, share, lead),...  38.6 us
    unnamed x10, local copies, waits for them, and re-layouts  5.02 us

profile of v5, /device:TPU:1, one launch (start us, length us, event | category | flops | bytes accessed | tf_op | source)
XLA Modules:
  0.0 44.2 jit_solution(16078105927216420861)
XLA Ops:
  0.6 38.6 %shard_map.84 = (bf16[256,2048]{1,0:T(8,128)(2,1)}, bf16[256,2048]{1,0:T(8,128)(2,1)}, bf16[256,256]{1,0:T(8,128)(2,1)}, bf16[256,256]{1,0:T(8,128)(2,1)}) custom-call(s32[16]{0:T(128)} %lengths.1, bf16[256,2048]{1,0:T(8,128)(2,1)} %query_hbm.1, bf16[256,256]{1,0:T(8,128)(2,1)} %keys.1, bf16[256,256]{1,0:T(8,128)(2,1)} %values.1, bf16[256,2048]{1,0:T(8,128)(2,1)} %grad_hbm.1), custom_call_target="tpu_custom_call" | custom-call | tf_op jit(solution)/shard_map/pallas_call | solution.py:323
  39.2 0.0 copy-start
  39.2 2.4 %copy.13 = bf16[256,2048]{1,0:T(8,128)(2,1)} copy(bf16[256,2048]{1,0:T(8,128)(2,1)} %get-tuple-element.8) | data formatting | bytes 2097152
  41.6 0.0 copy-done
  41.6 0.0 copy-start.2
  41.6 1.0 %copy.14 = bf16[256,2048]{1,0:T(8,128)(2,1)} copy(bf16[256,2048]{1,0:T(8,128)(2,1)S(1)} %copy-done) | data formatting | bytes 2097152
  42.6 0.1 copy-done.2
  42.6 0.0 copy-start.1
  42.6 0.7 %copy.15 = bf16[256,256]{1,0:T(8,128)(2,1)} copy(bf16[256,256]{1,0:T(8,128)(2,1)S(1)} %copy-done.2) | data formatting | bytes 262144
  43.3 0.3 copy-done.1
  43.6 0.7 %copy.16 = bf16[256,256]{1,0:T(8,128)(2,1)} copy(bf16[256,256]{1,0:T(8,128)(2,1)S(1)} %copy-done.1) | data formatting | bytes 262144
Async XLA Ops:
  39.2 2.4 %copy-start = (bf16[256,2048]{1,0:T(8,128)(2,1)S(1)}, bf16[256,2048]{1,0:T(8,128)(2,1)}, u32[]{:S(2)}) copy-start(bf16[256,2048]{1,0:T(8,128)(2,1)} %get-tuple-element.9) | copy-start | bytes 3145732
  41.6 1.0 %copy-start.2 = (bf16[256,256]{1,0:T(8,128)(2,1)S(1)}, bf16[256,256]{1,0:T(8,128)(2,1)}, u32[]{:S(2)}) copy-start(bf16[256,256]{1,0:T(8,128)(2,1)} %get-tuple-element.10) | copy-start | bytes 393220
  42.6 1.0 %copy-start.1 = (bf16[256,256]{1,0:T(8,128)(2,1)S(1)}, bf16[256,256]{1,0:T(8,128)(2,1)}, u32[]{:S(2)}) copy-start(bf16[256,256]{1,0:T(8,128)(2,1)} %get-tuple-element.11) | copy-start | bytes 393220
